TPU v7x, 256 devices: a whole 4x4x8 slice. The times are simulated.
256 devices in a mesh: seq: 32 (over z_lo, y, core), batch: 8 (over x, z_hi).
Axes of the slice: x: 4, y: 4, z: 8 (z_hi: 2, z_lo: 4; z = z_hi * 4 + z_lo), core: 2. Of those that a mesh axis runs over, the one named last changes fastest.
Arguments:
- coarse: bfloat16 [8, 8192, 1536], P('batch', 'seq'), may hold values from -6 to 6
- skip: bfloat16 [8, 16384, 1536], P('batch', 'seq'), may hold values from -6 to 6
- depth_kernel: float32 [3, 1536], replicated, may hold values from -3.5 to 3.5
- sep_weight: bfloat16 [1536, 1536], P('seq'), may hold values from -0.15625 to 0.15625
- sep_bias: float32 [1536], replicated, may hold values from -3 to 3
- head_weight: bfloat16 [1536, 3840], P(None, 'seq'), may hold values from -0.15625 to 0.15625
- head_bias: float32 [3840], replicated, may hold values from -4 to 4
- strand_pair: int32 [3840], replicated, may hold values from 0 to 3839, as said below
Outputs:
- preds: bfloat16 [8, 16384, 3840], P('batch', 'seq')
Inputs may be any that keep to these rules, and one draw needn't show every extreme that they name: strand_pair is a permutation with strand_pair[strand_pair[t]] == t; about half of the tracks are paired with another one.
All inputs are finite; a program needn't handle non-finite values.
Results may differ from a plain program's by a relative error of at most 0.0053.
Values may be sent and summed in bfloat16 or wider, within the bound.
A program may use at most 64 MiB of HBM per device.

v0:
```python
import jax
import jax.numpy as jnp
from jax import lax
from jax.sharding import PartitionSpec as P


def with_halo(cells, axis, width):
    count = lax.axis_size(axis)
    ends = count - 1
    head = lax.slice_in_dim(cells, 0, width, axis=0)
    tail = lax.slice_in_dim(cells, cells.shape[0] - width, cells.shape[0], axis=0)
    return jnp.concatenate(
        [
            lax.ppermute(tail, axis, [(i, (i + 1) % count) for i in range(ends)]),
            cells,
            lax.ppermute(head, axis, [((i + 1) % count, i) for i in range(ends)]),
        ],
        axis=0,
    )


def reversed_rows(x):
    rows = x.shape[0]
    r = lax.broadcasted_iota(jnp.int32, (rows, rows), 0)
    c = lax.broadcasted_iota(jnp.int32, (rows, rows), 1)
    flip = (r + c == rows - 1).astype(x.dtype)
    return jnp.dot(flip, x, preferred_element_type=jnp.float32).astype(x.dtype)


def to_mirror(x):
    nb, ns = (lax.axis_size("batch"), lax.axis_size("seq"))
    half = nb // 2
    route = []
    for s in range(ns):
        for b in range(nb):
            mirror = (ns - 1 - s) * nb + (b + half) % nb
            route.append((s * nb + b, mirror))
    return lax.ppermute(x, ("seq", "batch"), route)


def per_device(
    coarse, skip, depth_kernel, sep_weight, sep_bias, head_weight, head_bias, strand_pair
):
    sep_full = lax.all_gather(sep_weight, "seq", axis=0, tiled=True)
    head_full = lax.all_gather(head_weight, "seq", axis=1, tiled=True)
    upsampled = jnp.repeat(coarse[0].astype(jnp.float32), 2, axis=0)
    merged = (upsampled + skip[0]).astype(jnp.bfloat16)
    padded = with_halo(merged, "seq", 1)
    depthwise = (
        depth_kernel[0] * padded[:-2]
        + depth_kernel[1] * padded[1:-1]
        + depth_kernel[2] * padded[2:]
    )
    depthwise = depthwise.astype(jnp.bfloat16)
    mirrored = to_mirror(reversed_rows(depthwise))

    def head(block):
        pointwise = jnp.dot(block, sep_full, preferred_element_type=jnp.float32)
        features = jax.nn.gelu(pointwise + sep_bias, approximate=True).astype(jnp.bfloat16)
        logits = jnp.dot(features, head_full, preferred_element_type=jnp.float32)
        return jax.nn.softplus(logits + head_bias).astype(jnp.bfloat16)

    own = head(depthwise)
    other = jnp.take(head(mirrored), strand_pair, axis=1)
    averaged = 0.5 * (own.astype(jnp.float32) + other.astype(jnp.float32))
    return averaged.astype(jnp.bfloat16)[None]


def solution(mesh):
    in_specs = (
        P("batch", "seq", None),
        P("batch", "seq", None),
        P(),
        P("seq", None),
        P(),
        P(None, "seq"),
        P(),
        P(),
    )
    return jax.shard_map(
        per_device, mesh=mesh, in_specs=in_specs, out_specs=P("batch", "seq", None), check_vma=False
    )
```

profile of v0, /device:TPU:1, one launch (start us, length us, event | category | flops | bytes accessed | tf_op | source)
XLA Modules:
  0.0 285.9 jit_solution(13165414521046507312)
XLA Ops:
  6.5 0.0 all-gather.3.cloned.1.call-start
  6.5 0.7 all-gather.3.cloned.1.call-update
  7.3 0.0 all-gather.5.cloned.1.call-start
  7.3 0.7 all-gather.5.cloned.1.call-update
  8.0 1.3 bitcast_convert_fusion
  9.3 1.1 broadcast_in_dim.22
  10.4 3.3 %reshape.14 = f32[512,1536]{1,0:T(8,128)} reshape(f32[256,2,1536]{2,1,0:T(2,128)S(1)} %broadcast_in_dim.22) | data formatting | bytes 6291456 | tf_op jit(solution)/shard_map/reshape | solution.py:46
  13.7 0.0 copy-start.1
  13.7 2.8 fusion.19
  16.6 4.6 %collective-permute-start = (bf16[1,1536]{1,0:T(2,128)(2,1)S(1)}, bf16[1,1536]{1,0:T(2,128)(2,1)S(1)}, u32[]{:S(2)}, u32[]{:S(2)}) collective-permute-start(bf16[1,1536]{1,0:T(2,128)(2,1)S(1)} %get-tuple-element.8), channel_id=1, source_target_pairs={{0,8},{8,16},{16,24},{24,32},{32,40},{40,48},{48,56},{56,64},{64,7... | collective-permute-start | bytes 9224 | tf_op jit(solution)/shard_map/ppermute | solution.py:14
  21.2 1.9 collective-permute-start.1
  23.1 0.0 copy-done.1
  23.1 0.1 slice_reduce_fusion.2
  23.2 0.0 collective-permute-done
  23.2 2.9 %collective-permute-done.1 = bf16[1,1536]{1,0:T(2,128)(2,1)S(1)} collective-permute-done((bf16[1,1536]{1,0:T(2,128)(2,1)S(1)}, bf16[1,1536]{1,0:T(2,128)(2,1)S(1)}, u32[]{:S(2)}, u32[]{:S(2)}) %collective-permute-start.1) | collective-permute-done | bytes 3104 | tf_op jit(solution)/shard_map/ppermute | solution.py:16
  26.1 0.0 copy-start
  26.1 0.0 copy-start.3
  26.1 1.5 convolution_convert_fusion
  27.7 8.3 %collective-permute-start.2 = (bf16[512,1536]{1,0:T(8,128)(2,1)S(1)}, bf16[512,1536]{1,0:T(8,128)(2,1)S(1)}, u32[]{:S(2)}, u32[]{:S(2)}) collective-permute-start(bf16[512,1536]{1,0:T(8,128)(2,1)S(1)} %convolution_convert_fusion), channel_id=1, source_target_pairs={{0,252},{1,253},{2,254},{3,255},{4,248},{5,249},{6,250},{7,251},{8... | collective-permute-start | bytes 4718600 | tf_op jit(solution)/shard_map/ppermute | solution.py:38
  35.9 0.0 copy-done
  36.0 0.0 copy-start.2
  36.0 39.6 %collective-permute-done.2 = bf16[512,1536]{1,0:T(8,128)(2,1)S(1)} collective-permute-done((bf16[512,1536]{1,0:T(8,128)(2,1)S(1)}, bf16[512,1536]{1,0:T(8,128)(2,1)S(1)}, u32[]{:S(2)}, u32[]{:S(2)}) %collective-permute-start.2) | collective-permute-done | bytes 1572896 | tf_op jit(solution)/shard_map/ppermute | solution.py:38
  75.6 64.0 %all-gather.3.cloned.1.call-done = bf16[1536,1536]{1,0:T(8,128)(2,1)} async-done(((bf16[48,1536]{1,0:T(8,128)(2,1)}), bf16[1536,1536]{1,0:T(8,128)(2,1)}) %all-gather.3.cloned.1.call-update) | async-done | bytes 4718608 | tf_op jit(solution)/shard_map/all_gather | solution.py:44
  139.6 0.0 copy-done.3
  139.6 6.6 %fusion.20 = bf16[512,1536]{1,0:T(8,128)(2,1)} fusion(bf16[512,1536]{1,0:T(8,128)(2,1)S(1)} %collective-permute-done.2, bf16[1536,1536]{1,0:T(8,128)(2,1)} %all-gather.3.cloned.1.call-done, f32[1536]{0:T(1024)S(1)} %copy-done.3), kind=kOutput, calls=%fused_computation.31 | convolution fusion | flops 2423783424 | bytes 7870464 | tf_op jit(solution)/shard_map/dot_general | solution.py:58
  146.2 70.0 %all-gather.5.cloned.1.call-done = bf16[1536,3840]{0,1:T(8,128)(2,1)} async-done(((bf16[1536,120]{0,1:T(8,128)(2,1)}), bf16[1536,3840]{0,1:T(8,128)(2,1)}) %all-gather.5.cloned.1.call-update) | async-done | bytes 11796496 | tf_op jit(solution)/shard_map/all_gather | solution.py:45
  216.2 0.0 copy-done.2
  216.2 15.1 %fusion.1 = bf16[512,3840]{1,0:T(8,128)(2,1)} fusion(bf16[512,1536]{1,0:T(8,128)(2,1)} %fusion.20, bf16[1536,3840]{0,1:T(8,128)(2,1)} %all-gather.5.cloned.1.call-done, f32[3840]{0:T(1024)S(1)} %copy-done.2), kind=kOutput, calls=%fused_computation.4 | convolution fusion | flops 6055526400 | bytes 17316864 | tf_op jit(solution)/shard_map/dot_general | solution.py:60
  231.4 6.3 %copy.9 = bf16[512,3840]{0,1:T(8,128)(2,1)} copy(bf16[512,3840]{1,0:T(8,128)(2,1)} %fusion.1) | data formatting | bytes 7864320 | tf_op jit(solution)/shard_map/convert_element_type | solution.py:61
  237.6 14.5 %gather_fusion = bf16[3840,512]{1,0:T(8,128)(2,1)} fusion(bf16[512,3840]{0,1:T(8,128)(2,1)} %copy.9, s32[4096]{0:T(1024)S(1)} %pad_clamp_fusion), kind=kCustom, calls=%fused_computation | custom fusion | bytes 7879680 | tf_op jit(solution)/shard_map/jit(_take)/gather | solution.py:64
  252.1 6.3 %copy.10 = bf16[3840,512]{0,1:T(8,128)(2,1)} copy(bf16[3840,512]{1,0:T(8,128)(2,1)} %gather_fusion) | data formatting | bytes 7864320 | tf_op jit(solution)/shard_map/jit(_take)/gather | solution.py:64
  258.4 20.7 %fusion.4 = bf16[1,512,3840]{2,1,0:T(8,128)(2,1)} fusion(bf16[1536,3840]{0,1:T(8,128)(2,1)} %all-gather.5.cloned.1.call-done, bf16[3840,512]{0,1:T(8,128)(2,1)} %copy.10, f32[3840]{0:T(1024)S(1)} %copy-done.2, pred[3840]{0:T(1024)(128)(4,1)S(1)} %compare_and_fusion, bf16[1536,1536]{1,0:T(8,128)(2,1)} %all-gather.3.cloned.1.call-done, ...), kind=kOutput, calls=%fused_computation.8 | convolution fusion | flops 8502902784 | bytes 26002176 | tf_op jit(solution)/shard_map/dot_general | solution.py:60
  (4 shorter events, 0.0 us)
Async XLA Ops:
  6.5 133.1 %all-gather.3.cloned.1.call-start = ((), (), s32[]{:S(2)}) async-start(), calls=%async_computation | async-start | bytes 4866048 | tf_op jit(solution)/shard_map/all_gather | solution.py:44
  7.3 209.0 %all-gather.5.cloned.1.call-start = ((), (), s32[]{:S(2)}) async-start(), calls=%async_computation.1 | async-start | bytes 12165120 | tf_op jit(solution)/shard_map/all_gather | solution.py:45
  13.7 9.4 %copy-start.1 = (f32[3,1536]{1,0:T(4,128)S(1)}, f32[3,1536]{1,0:T(4,128)}, u32[]{:S(2)}) copy-start(f32[3,1536]{1,0:T(4,128)} %param.10) | copy-start | bytes 55300
  16.6 6.6 %collective-permute-start = (bf16[1,1536]{1,0:T(2,128)(2,1)S(1)}, bf16[1,1536]{1,0:T(2,128)(2,1)S(1)}, u32[]{:S(2)}, u32[]{:S(2)}) collective-permute-start(bf16[1,1536]{1,0:T(2,128)(2,1)S(1)} %get-tuple-element.8), channel_id=1, source_target_pairs={{0,8},{8,16},{16,24},{24,32},{32,40},{40,48},{48,56},{56,64},{64,7... | collective-permute-start | bytes 9224 | tf_op jit(solution)/shard_map/ppermute | solution.py:14
  21.2 4.9 %collective-permute-start.1 = (bf16[1,1536]{1,0:T(2,128)(2,1)S(1)}, bf16[1,1536]{1,0:T(2,128)(2,1)S(1)}, u32[]{:S(2)}, u32[]{:S(2)}) collective-permute-start(bf16[1,1536]{1,0:T(2,128)(2,1)S(1)} %get-tuple-element.9), channel_id=1, source_target_pairs={{8,0},{16,8},{24,16},{32,24},{40,32},{48,40},{56,48},{64,56},{72,6... | collective-permute-start | bytes 9224 | tf_op jit(solution)/shard_map/ppermute | solution.py:16
  26.1 9.8 %copy-start = (s32[3840]{0:T(1024)S(1)}, s32[3840]{0:T(1024)}, u32[]{:S(2)}) copy-start(s32[3840]{0:T(1024)} %param.15) | copy-start | bytes 46084
  26.1 113.5 %copy-start.3 = (f32[1536]{0:T(1024)S(1)}, f32[1536]{0:T(1024)}, u32[]{:S(2)}) copy-start(f32[1536]{0:T(1024)} %param.12) | copy-start | bytes 18436
  27.7 48.0 %collective-permute-start.2 = (bf16[512,1536]{1,0:T(8,128)(2,1)S(1)}, bf16[512,1536]{1,0:T(8,128)(2,1)S(1)}, u32[]{:S(2)}, u32[]{:S(2)}) collective-permute-start(bf16[512,1536]{1,0:T(8,128)(2,1)S(1)} %convolution_convert_fusion), channel_id=1, source_target_pairs={{0,252},{1,253},{2,254},{3,255},{4,248},{5,249},{6,250},{7,251},{8... | collective-permute-start | bytes 4718600 | tf_op jit(solution)/shard_map/ppermute | solution.py:38
  36.0 180.3 %copy-start.2 = (f32[3840]{0:T(1024)S(1)}, f32[3840]{0:T(1024)}, u32[]{:S(2)}) copy-start(f32[3840]{0:T(1024)} %param.14) | copy-start | bytes 46084
Sparse Core Ops, SparseCore 0:
  9.2 130.4 all-gather.2
  141.5 74.6 all-gather.4
where the time goes:
time: 286 us
  waiting for transfers between devices  178 us (62%)
  matrix products  44 us (15%)
  local copies, waits for them, and re-layouts  31.5 us (11%)
  starting transfers between devices  14.8 us (5%)
  between operations  13.5 us (5%)
  other arithmetic  4.14 us (1%)
    all_gather x1, waiting for transfers between devices, per_device(): head_full = lax.all_gather(head_weight, 'seq', axis=1, tiled=True)  70 us
    all_gather x1, waiting for transfers between devices, per_device(): sep_full = lax.all_gather(sep_weight, 'seq', axis=0, tiled=True)  64 us
    ppermute x1, waiting for transfers between devices, to_mirror(): return lax.ppermute(x, ('seq', 'batch'), route)  39.6 us
    dot_general x2, matrix products, head(): logits = jnp.dot(features, head_full, preferred_element_type=jnp.float32)  35.8 us
    gather x2, local copies, waits for them, and re-layouts, per_device(): other = jnp.take(head(mirrored), strand_pair, axis=1)  20.7 us
    ppermute x1, starting transfers between devices, to_mirror(): return lax.ppermute(x, ('seq', 'batch'), route)  8.27 us
    dot_general x1, matrix products, head(): pointwise = jnp.dot(block, sep_full, preferred_element_type=jnp.float32)  6.6 us
    convert_element_type x1, local copies, waits for them, and re-layouts, head(): return jax.nn.softplus(logits + head_bias).astype(jnp.bfloat16)  6.29 us
  transfers between devices with their start and end apart: 5, of which 4 were waited for; matrix products, arithmetic and copies ran while one was open for 6% of the time, Pallas kernels for 0%

commit v1 on v0

--- a/solution.py
+++ b/solution.py
@@ -42,7 +42,9 @@
     coarse, skip, depth_kernel, sep_weight, sep_bias, head_weight, head_bias, strand_pair
 ):
     sep_full = lax.all_gather(sep_weight, "seq", axis=0, tiled=True)
-    head_full = lax.all_gather(head_weight, "seq", axis=1, tiled=True)
+    head_full = jnp.concatenate(
+        lax.all_to_all(jnp.stack([head_weight] * lax.axis_size("seq")), "seq", 0, 0), axis=1
+    )
     upsampled = jnp.repeat(coarse[0].astype(jnp.float32), 2, axis=0)
     merged = (upsampled + skip[0]).astype(jnp.bfloat16)
     padded = with_halo(merged, "seq", 1)

time: 286 us -> 453 us (1.58)
  the two profiles are of different devices: /device:TPU:1 before, /device:TPU:57 now
where the time goes in v1:
time: 453 us; the launch traced here: 452 us
  waiting for transfers between devices  335 us (74%)
  matrix products  44 us (10%)
  local copies, waits for them, and re-layouts  37.5 us (8%)
  starting transfers between devices  19.5 us (4%)
  between operations  13.5 us (3%)
    ppermute x1, waiting for transfers between devices, with_halo(): lax.ppermute(head, axis, [((i + 1) % count, i) for i in range(ends)])  303 us
    dot_general x2, matrix products, head(): logits = jnp.dot(features, head_full, preferred_element_type=jnp.float32)  35.8 us
    ppermute x1, waiting for transfers between devices, to_mirror(): return lax.ppermute(x, ('seq', 'batch'), route)  31.4 us
    gather x2, local copies, waits for them, and re-layouts, per_device(): other = jnp.take(head(mirrored), strand_pair, axis=1)  20.7 us
  transfers between devices with their start and end apart: 5, of which 2 were waited for; matrix products, arithmetic and copies ran while one was open for 3% of the time, Pallas kernels for 0%

profile of v1, /device:TPU:57, one launch (start us, length us, event | category | flops | bytes accessed | tf_op | source)
XLA Modules:
  0.0 452.4 jit_solution(5771915756916947681)
XLA Ops:
  6.5 6.0 %stack.2 = bf16[32,1536,120]{1,2,0:T(8,128)(2,1)} broadcast(bf16[1536,120]{0,1:T(8,128)(2,1)} %param.13), dimensions={1,2} | broadcast | bytes 12165120 | tf_op jit(solution)/shard_map/stack | solution.py:46
  12.5 0.0 copy-start
  12.6 8.9 %all-to-all-start = ((bf16[32,1536,120]{1,2,0:T(8,128)(2,1)}), bf16[32,1536,120]{1,2,0:T(8,128)(2,1)}, u32[]{:S(2)}, u32[]{:S(2)}) async-start(bf16[32,1536,120]{1,2,0:T(8,128)(2,1)} %stack.2), calls=%async_computation | async-start | bytes 23592960 | tf_op jit(solution)/shard_map/all_to_all | solution.py:46
  21.5 0.0 all-gather.2.cloned.1.call-start
  21.5 0.7 all-gather.2.cloned.1.call-update
  22.2 0.0 copy-done
  22.2 0.2 bitcast_convert_fusion
  22.4 1.1 broadcast_in_dim.22
  23.5 3.3 reshape.22
  26.8 0.0 copy-start.2
  26.8 2.8 fusion.19
  29.7 2.3 collective-permute-start.1
  32.0 5.4 %collective-permute-start = (bf16[1,1536]{1,0:T(2,128)(2,1)S(1)}, bf16[1,1536]{1,0:T(2,128)(2,1)S(1)}, u32[]{:S(2)}, u32[]{:S(2)}) collective-permute-start(bf16[1,1536]{1,0:T(2,128)(2,1)S(1)} %get-tuple-element.8), channel_id=1, source_target_pairs={{0,8},{8,16},{16,24},{24,32},{32,40},{40,48},{48,56},{56,64},{64,7... | collective-permute-start | bytes 9224 | tf_op jit(solution)/shard_map/ppermute | solution.py:14
  37.4 0.0 copy-done.2
  37.4 0.1 slice_reduce_fusion.2
  37.4 302.9 %collective-permute-done.1 = bf16[1,1536]{1,0:T(2,128)(2,1)S(1)} collective-permute-done((bf16[1,1536]{1,0:T(2,128)(2,1)S(1)}, bf16[1,1536]{1,0:T(2,128)(2,1)S(1)}, u32[]{:S(2)}, u32[]{:S(2)}) %collective-permute-start.1) | collective-permute-done | bytes 3104 | tf_op jit(solution)/shard_map/ppermute | solution.py:16
  340.3 0.0 collective-permute-done
  340.3 0.0 copy-start.1
  340.3 0.0 copy-start.4
  340.3 1.5 convolution_convert_fusion
  341.9 2.9 collective-permute-start.2
  344.7 0.0 copy-done.1
  344.8 0.0 copy-start.3
  344.8 31.4 %collective-permute-done.2 = bf16[512,1536]{1,0:T(8,128)(2,1)S(1)} collective-permute-done((bf16[512,1536]{1,0:T(8,128)(2,1)S(1)}, bf16[512,1536]{1,0:T(8,128)(2,1)S(1)}, u32[]{:S(2)}, u32[]{:S(2)}) %collective-permute-start.2) | collective-permute-done | bytes 1572896 | tf_op jit(solution)/shard_map/ppermute | solution.py:38
  376.1 0.0 all-gather.2.cloned.1.call-done
  376.1 0.0 copy-done.4
  376.2 6.6 %fusion.20 = bf16[512,1536]{1,0:T(8,128)(2,1)} fusion(bf16[512,1536]{1,0:T(8,128)(2,1)S(1)} %collective-permute-done.2, bf16[1536,1536]{1,0:T(8,128)(2,1)} %all-gather.2.cloned.1.call-done, f32[1536]{0:T(1024)S(1)} %copy-done.4), kind=kOutput, calls=%fused_computation.31 | convolution fusion | flops 2423783424 | bytes 7870464 | tf_op jit(solution)/shard_map/dot_general | solution.py:60
  382.8 0.0 all-to-all-done
  382.8 0.0 copy-done.3
  382.8 15.1 %fusion.1 = bf16[512,3840]{1,0:T(8,128)(2,1)} fusion(bf16[512,1536]{1,0:T(8,128)(2,1)} %fusion.20, bf16[1536,3840]{0,1:T(8,128)(2,1)} %bitcast.3, f32[3840]{0:T(1024)S(1)} %copy-done.3), kind=kOutput, calls=%fused_computation.4 | convolution fusion | flops 6055526400 | bytes 17316864 | tf_op jit(solution)/shard_map/dot_general | solution.py:62
  397.9 6.3 %copy.12 = bf16[512,3840]{0,1:T(8,128)(2,1)} copy(bf16[512,3840]{1,0:T(8,128)(2,1)} %fusion.1) | data formatting | bytes 7864320 | tf_op jit(solution)/shard_map/convert_element_type | solution.py:63
  404.2 14.5 %gather_fusion = bf16[3840,512]{1,0:T(8,128)(2,1)} fusion(bf16[512,3840]{0,1:T(8,128)(2,1)} %copy.12, s32[4096]{0:T(1024)S(1)} %pad_clamp_fusion), kind=kCustom, calls=%fused_computation | custom fusion | bytes 7879680 | tf_op jit(solution)/shard_map/jit(_take)/gather | solution.py:66
  418.7 6.2 %copy.13 = bf16[3840,512]{0,1:T(8,128)(2,1)} copy(bf16[3840,512]{1,0:T(8,128)(2,1)} %gather_fusion) | data formatting | bytes 7864320 | tf_op jit(solution)/shard_map/jit(_take)/gather | solution.py:66
  424.9 20.7 %fusion.4 = bf16[1,512,3840]{2,1,0:T(8,128)(2,1)} fusion(bf16[1536,3840]{0,1:T(8,128)(2,1)} %bitcast.3, bf16[3840,512]{0,1:T(8,128)(2,1)} %copy.13, f32[3840]{0:T(1024)S(1)} %copy-done.3, pred[3840]{0:T(1024)(128)(4,1)S(1)} %compare_and_fusion, bf16[1536,1536]{1,0:T(8,128)(2,1)} %all-gather.2.cloned.1.call-done, f32[1536]{0:T(1024)S(1)} %copy-done.4, ...), kind=kOutput, calls=%fused_computation.8 | convolution fusion | flops 8502902784 | bytes 26002176 | tf_op jit(solution)/shard_map/dot_general | solution.py:62
  (4 shorter events, 0.0 us)
Async XLA Ops:
  12.5 9.7 %copy-start = (bf16[1,256,1536]{2,1,0:T(8,128)(2,1)S(1)}, bf16[1,256,1536]{2,1,0:T(8,128)(2,1)}, u32[]{:S(2)}) copy-start(bf16[1,256,1536]{2,1,0:T(8,128)(2,1)} %param.8) | copy-start | bytes 2359300
  12.6 370.2 %all-to-all-start = ((bf16[32,1536,120]{1,2,0:T(8,128)(2,1)}), bf16[32,1536,120]{1,2,0:T(8,128)(2,1)}, u32[]{:S(2)}, u32[]{:S(2)}) async-start(bf16[32,1536,120]{1,2,0:T(8,128)(2,1)} %stack.2), calls=%async_computation | async-start | bytes 23592960 | tf_op jit(solution)/shard_map/all_to_all | solution.py:46
  21.5 354.7 %all-gather.2.cloned.1.call-start = ((), (), s32[]{:S(2)}) async-start(), calls=%async_computation.1 | async-start | bytes 4866048 | tf_op jit(solution)/shard_map/all_gather | solution.py:44
  26.8 10.5 %copy-start.2 = (f32[3,1536]{1,0:T(4,128)S(1)}, f32[3,1536]{1,0:T(4,128)}, u32[]{:S(2)}) copy-start(f32[3,1536]{1,0:T(4,128)} %param.10) | copy-start | bytes 55300
  29.7 310.7 %collective-permute-start.1 = (bf16[1,1536]{1,0:T(2,128)(2,1)S(1)}, bf16[1,1536]{1,0:T(2,128)(2,1)S(1)}, u32[]{:S(2)}, u32[]{:S(2)}) collective-permute-start(bf16[1,1536]{1,0:T(2,128)(2,1)S(1)} %get-tuple-element.9), channel_id=1, source_target_pairs={{8,0},{16,8},{24,16},{32,24},{40,32},{48,40},{56,48},{64,56},{72,6... | collective-permute-start | bytes 9224 | tf_op jit(solution)/shard_map/ppermute | solution.py:16
  32.0 308.3 %collective-permute-start = (bf16[1,1536]{1,0:T(2,128)(2,1)S(1)}, bf16[1,1536]{1,0:T(2,128)(2,1)S(1)}, u32[]{:S(2)}, u32[]{:S(2)}) collective-permute-start(bf16[1,1536]{1,0:T(2,128)(2,1)S(1)} %get-tuple-element.8), channel_id=1, source_target_pairs={{0,8},{8,16},{16,24},{24,32},{32,40},{40,48},{48,56},{56,64},{64,7... | collective-permute-start | bytes 9224 | tf_op jit(solution)/shard_map/ppermute | solution.py:14
  340.3 4.4 copy-start.1
  340.3 35.8 %copy-start.4 = (f32[1536]{0:T(1024)S(1)}, f32[1536]{0:T(1024)}, u32[]{:S(2)}) copy-start(f32[1536]{0:T(1024)} %param.12) | copy-start | bytes 18436
  341.9 34.3 %collective-permute-start.2 = (bf16[512,1536]{1,0:T(8,128)(2,1)S(1)}, bf16[512,1536]{1,0:T(8,128)(2,1)S(1)}, u32[]{:S(2)}, u32[]{:S(2)}) collective-permute-start(bf16[512,1536]{1,0:T(8,128)(2,1)S(1)} %convolution_convert_fusion), channel_id=1, source_target_pairs={{0,252},{1,253},{2,254},{3,255},{4,248},{5,249},{6,250},{7,251},{8... | collective-permute-start | bytes 4718600 | tf_op jit(solution)/shard_map/ppermute | solution.py:38
  344.8 38.0 %copy-start.3 = (f32[3840]{0:T(1024)S(1)}, f32[3840]{0:T(1024)}, u32[]{:S(2)}) copy-start(f32[3840]{0:T(1024)} %param.14) | copy-start | bytes 46084
Sparse Core Ops, SparseCore 0:
  24.1 167.7 all-gather.1
